TPU v7x, 256 devices: a whole 4x4x8 slice. The times are simulated.
256 devices in a mesh: grp: 8 (over z), sub: 32 (over x, y, core).
Axes of the slice: x: 4, y: 4, z: 8, core: 2. Of those that a mesh axis runs over, the one named last changes fastest.
Arguments:
- residual: float32 [16, 98304], P(None, 'sub'), may hold values from -6 to 6
- margin: int32 [32, 8], replicated, may hold values from 0 to 767, as said below
- aggregate: int32 [768], P('sub'), may hold values from 0 to 63
- local_factor: bfloat16 [32, 4096, 4096], P('sub', 'grp'), may hold values from -0.09375 to 0.09375
- coarse_factor: bfloat16 [8192, 8192], P('sub'), may hold values from -0.0625 to 0.0625
Outputs:
- preconditioned: float32 [16, 98304], P('grp', 'sub')
Inputs may be any that keep to these rules, and one draw needn't show every extreme that they name: `margin`: for subdomain s, every entry names a block owned by another subdomain (block b is owned by subdomain b // 24); the entries of one row are distinct. Up to 8 entries of one row may name blocks of the same owner, and in every draw some row takes all of its entries from a single owner. `aggregate`: the counts of global blocks for each coarse block are whole numbers and may cross devices as int32.
All inputs are finite; a program needn't handle non-finite values.
Results may differ from a plain program's by a relative error of at most 0.0033.
Values sent between devices are 32-bit elements; how exact they have to be, the bound alone decides.
A program may use at most 64 MiB of HBM per device.

v0:
```python
import jax
import jax.numpy as jnp
from jax import lax
from jax.sharding import PartitionSpec as P

BLK = 128
NCB = 64


def row_of(table, index):
    return lax.dynamic_index_in_dim(table, index, 0, keepdims=False)


def on_device(residual, margin, aggregate, local_factor, coarse_factor):
    sub_count = lax.axis_size("sub")
    grp_count = lax.axis_size("grp")
    my_index = lax.axis_index("sub")
    grp_index = lax.axis_index("grp")
    rhs_count, own_width = residual.shape
    owned = own_width // BLK
    group_rows = rhs_count // grp_count
    blocks = residual.reshape(rhs_count, owned, BLK)
    exact = lax.Precision.HIGHEST
    my_list = row_of(margin, my_index)
    all_blocks = jnp.arange(owned * sub_count, dtype=jnp.int32)
    selector = (my_list[:, None] == all_blocks[None, :]).astype(jnp.float32)
    whole = lax.all_gather(blocks, "sub", axis=1, tiled=True)
    halo_rows = jnp.einsum("kb,rbc->rkc", selector, whole, precision=exact)
    local_rhs = (
        jnp.concatenate([blocks, halo_rows], axis=1).reshape(rhs_count, -1).astype(jnp.bfloat16)
    )
    factor = local_factor[0]
    inner_term = jnp.dot(local_rhs, factor.T, preferred_element_type=jnp.float32).astype(
        jnp.bfloat16
    )
    local_sol = lax.psum_scatter(
        jnp.dot(inner_term, factor, preferred_element_type=jnp.float32),
        "grp",
        scatter_dimension=0,
        tiled=True,
    )
    local_sol = local_sol.reshape(group_rows, -1, BLK)
    own_part = local_sol[:, :owned]
    back_rows = local_sol[:, owned:]
    spread = jnp.einsum("kb,rkc->rbc", selector, back_rows, precision=exact)
    returned = lax.psum_scatter(spread, "sub", scatter_dimension=1, tiled=True)
    catalog = jnp.arange(NCB, dtype=jnp.int32)
    member = (aggregate[:, None] == catalog[None, :]).astype(jnp.float32)
    mine = lax.dynamic_slice_in_dim(blocks, grp_index * group_rows, group_rows, 0)
    sums_part = jnp.einsum("rbk,bj->rjk", mine, member, precision=exact)
    sums, counts = lax.psum((sums_part, jnp.sum(member, axis=0)), "sub")
    coarse_rhs = (
        (sums / jnp.maximum(counts, 1.0)[None, :, None])
        .reshape(group_rows, -1)
        .astype(jnp.bfloat16)
    )
    inner_coarse = jnp.dot(coarse_rhs, coarse_factor.T, preferred_element_type=jnp.float32).astype(
        jnp.bfloat16
    )
    coarse_part = jnp.dot(inner_coarse, coarse_factor, preferred_element_type=jnp.float32)
    coarse_sol = lax.psum(coarse_part, "sub")
    prolonged = jnp.einsum(
        "rjk,bj->rbk", coarse_sol.reshape(group_rows, NCB, BLK), member, precision=exact
    )
    result = own_part + returned + prolonged
    return result.reshape(group_rows, -1)


def solution(mesh):
    placed = (P(None, "sub"), P(), P("sub"), P("sub", "grp", None), P("sub", None))
    return jax.shard_map(
        on_device, mesh=mesh, in_specs=placed, out_specs=P("grp", "sub"), check_vma=False
    )
```

profile of v0, /device:TPU:1, one launch (start us, length us, event | category | flops | bytes accessed | tf_op | source)
XLA Modules:
  0.0 459.4 jit_solution(2734043562929597561)
XLA Ops:
  6.5 0.0 copy-start
  6.5 1.0 copy.9
  7.5 1.6 convolution_bitcast_fusion.2
  9.2 0.0 all-reduce.5.cloned.1.call-update
  9.2 0.0 all-gather.2.cloned.1.call-start
  9.2 0.7 all-gather.2.cloned.1.call-update
  9.9 0.0 all-reduce.9.cloned.1.call-start
  10.0 0.2 dynamic-slice_reduce_fusion
  10.2 1.3 dynamic-slice
  12.1 0.7 convert_reduce_fusion
  12.8 65.2 %psum.22 = f32[64]{0:T(128)S(1)} all-reduce(f32[64]{0:T(128)S(1)} %convert_reduce_fusion), channel_id=1, replica_groups=mesh['grp'=8,'sub'=32] {'sub'}, use_global_device_ids=true, to_apply=%region_4.5 | all-reduce | flops 64 | bytes 512 | tf_op jit(solution)/shard_map/psum | solution.py:51
  78.1 0.9 bitcast_convert_fusion
  79.0 42.9 %all-reduce.5.cloned.1.call-done = f32[2,64,128]{2,1,0:T(8,128)} async-done(((f32[2,64,128]{2,1,0:T(8,128)}), f32[2,64,128]{2,1,0:T(8,128)}) %all-reduce.5.cloned.1.call-update) | async-done | bytes 65552 | tf_op jit(solution)/shard_map/psum | solution.py:51
  122.0 0.9 fusion.20
  122.9 55.0 %all-gather.2.cloned.1.call-done = f32[16,768,128]{2,1,0:T(8,128)} async-done(((f32[16,24,128]{2,1,0:T(8,128)}), f32[16,768,128]{2,1,0:T(8,128)}) %all-gather.2.cloned.1.call-update) | async-done | bytes 6291472 | tf_op jit(solution)/shard_map/all_gather | solution.py:27
  177.9 4.8 %fusion.4 = bf16[16,8,128]{2,1,0:T(8,128)(2,1)S(1)} fusion(f32[16,768,128]{2,1,0:T(8,128)} %all-gather.2.cloned.1.call-done, s32[8]{0:T(128)S(1)} %dynamic-slice_reduce_fusion), kind=kOutput, calls=%fused_computation.8 | convolution fusion | flops 151017472 | bytes 6324256 | tf_op jit(solution)/shard_map/kb,rbc->rkc/dot_general | solution.py:28
  182.8 6.0 %fusion = f32[16,4096]{1,0:T(8,128)} fusion(bf16[1,512,4096]{2,1,0:T(8,128)(2,1)} %param.8, bf16[2,8,32,128]{3,2,1,0:T(8,128)(2,1)S(1)} %bitcast.65), kind=kOutput, calls=%fused_computation | convolution fusion | flops 134225920 | bytes 4587520 | tf_op jit(solution)/shard_map/dot_general | solution.py:37
  188.8 0.0 all-reduce.9.cloned.1.call-update
  188.8 0.0 copy-start.2
  188.8 0.0 all-reduce.7.cloned.1.call-start
  188.9 6.4 %convolution_bitcast_fusion.1 = f32[1,2,64,128]{3,1,2,0:T(2,128)S(1)} fusion(bf16[256,8192]{1,0:T(8,128)(2,1)} %param.9, bf16[1,2,64,128]{3,2,1,0:T(8,128)(2,1)S(1)} %fusion.20), kind=kOutput, calls=%fused_computation.5 | convolution fusion | flops 16777728 | bytes 4292608 | tf_op jit(solution)/shard_map/dot_general | solution.py:60
  195.2 0.6 copy.28
  195.8 0.0 all-reduce.7.cloned.1.call-update
  195.9 0.0 reduce-scatter.2.cloned.1.call-start
  195.9 59.3 %all-reduce.9.cloned.1.call-done = f32[16,4096]{1,0:T(8,128)} async-done(((f32[16,4096]{1,0:T(8,128)}), f32[16,4096]{1,0:T(8,128)}) %all-reduce.9.cloned.1.call-update) | async-done | bytes 262160
  255.2 0.9 dynamic-slice_bitcast_fusion
  256.1 1.5 convolution_bitcast_fusion
  257.6 0.0 reduce-scatter.2.cloned.1.call-update
  257.6 111.8 %all-reduce.7.cloned.1.call-done = f32[2,64,128]{2,1,0:T(8,128)} async-done(((f32[2,64,128]{2,1,0:T(8,128)}), f32[2,64,128]{2,1,0:T(8,128)}) %all-reduce.7.cloned.1.call-update) | async-done | bytes 65552 | tf_op jit(solution)/shard_map/psum | solution.py:61
  369.4 81.8 %reduce-scatter.2.cloned.1.call-done = f32[2,24,128]{2,1,0:T(8,128)} async-done(((f32[2,768,128]{2,1,0:T(8,128)}), f32[2,24,128]{2,1,0:T(8,128)}) %reduce-scatter.2.cloned.1.call-update) | async-done | bytes 24592 | tf_op jit(solution)/shard_map/reduce_scatter | solution.py:46
  451.2 1.0 fusion.11
  452.3 0.6 copy.30
  (8 shorter events, 0.0 us)
Async XLA Ops:
  6.5 3.5 copy-start
  6.5 115.4 %all-reduce.5.cloned.1.call-start = ((), (), s32[]{:S(2)}) async-start(), calls=%async_computation.3 | async-start | bytes 131072 | tf_op jit(solution)/shard_map/psum | solution.py:51
  7.5 1.7 copy-start.1
  9.2 168.7 %all-gather.2.cloned.1.call-start = ((), (), s32[]{:S(2)}) async-start(), calls=%async_computation.1 | async-start | bytes 6488064 | tf_op jit(solution)/shard_map/all_gather | solution.py:27
  9.9 245.2 %all-reduce.9.cloned.1.call-start = ((), (), s32[]{:S(2)}) async-start(), calls=%async_computation.5 | async-start | bytes 524288
  188.8 262.4 %copy-start.2 = (s32[24]{0:T(128)S(1)}, s32[24]{0:T(128)}, u32[]{:S(2)}) copy-start(s32[24]{0:T(128)} %param.7) | copy-start | bytes 292
  188.8 180.6 %all-reduce.7.cloned.1.call-start = ((), (), s32[]{:S(2)}) async-start(), calls=%async_computation.4 | async-start | bytes 131072 | tf_op jit(solution)/shard_map/psum | solution.py:61
  195.9 255.3 %reduce-scatter.2.cloned.1.call-start = ((), (), s32[]{:S(2)}) async-start(), calls=%async_computation.2 | async-start | bytes 811008 | tf_op jit(solution)/shard_map/reduce_scatter | solution.py:46
Sparse Core Ops, SparseCore 0:
  10.6 111.3 all-reduce.4
  124.6 53.2 all-gather.1
  188.9 66.2 all-reduce.8
  258.3 111.0 all-reduce.6
  373.1 78.1 reduce-scatter.1
where the time goes:
time: 460 us; the launch traced here: 459 us
  waiting for transfers between devices  352 us (77%)
  blocking collectives  65.2 us (14%)
  matrix products  21.3 us (5%)
  between operations  13.9 us (3%)
  local copies, waits for them, and re-layouts  4.62 us (1%)
    psum x1, waiting for transfers between devices, on_device(): coarse_sol = lax.psum(coarse_part, 'sub')  112 us
    reduce_scatter x1, waiting for transfers between devices, on_device(): returned = lax.psum_scatter(spread, 'sub', scatter_dimension=1, tiled=True)  81.8 us
    psum x1, blocking collectives, on_device(): sums, counts = lax.psum((sums_part, jnp.sum(member, axis=0)), 'sub')  65.2 us
    unnamed x6, waiting for transfers between devices  60 us
    all_gather x1, waiting for transfers between devices, on_device(): whole = lax.all_gather(blocks, 'sub', axis=1, tiled=True)  55 us
    psum x1, waiting for transfers between devices, on_device(): sums, counts = lax.psum((sums_part, jnp.sum(member, axis=0)), 'sub')  42.9 us
  transfers between devices with their start and end apart: 5, of which 5 were waited for; matrix products, arithmetic and copies ran while one was open for 3% of the time, Pallas kernels for 0%

commit v1 on v0

v1 whole, which is shorter than its diff:
```python
import functools

import jax
import jax.numpy as jnp
from jax import lax
from jax.experimental import pallas as pl
from jax.experimental.pallas import tpu as pltpu
from jax.sharding import PartitionSpec as P

BLK = 128
F32 = jnp.float32
BF16 = jnp.bfloat16
MESH = pl.DeviceIdType.MESH
NT = (((1,), (1,)), ((), ()))


def split_dot(onehot, values):
    high = values.astype(BF16)
    low = (values - high.astype(F32)).astype(BF16)
    return jnp.dot(onehot, high, preferred_element_type=F32) + jnp.dot(
        onehot, low, preferred_element_type=F32
    )


def wait_all(ref, sem):
    pltpu.make_async_copy(ref, ref, sem).wait()


def kernel(
    sizes,
    margin, aggregate, residual, local_factor, coarse_factor,
    out,
    res_v, w_v, v_v, gathered, pick_out, pick_in, sums_out, sums_in, halo, c_rows,
    part_h, recv_h, part_o, recv_o, back, e_part, e_recv, e_full, acc,
    load_sem, gather_send, gather_recv, pair_send, pair_recv, halo_send, halo_recv,
    h_send, h_recv, o_send, o_recv, back_send, back_recv, es_send, es_recv, ea_send, ea_recv,
):
    n_sub, n_grp, own, margins, ncb = sizes
    nq = n_sub // 2
    rows = 2
    per = ncb // n_sub
    me = lax.axis_index("sub")
    grp = lax.axis_index("grp")
    core = lax.rem(me, 2)
    q = lax.div(me, 2)
    pair = me + 1 - 2 * core

    for b in range(own):
        pltpu.make_async_copy(
            residual.at[:, pl.ds(b * BLK, BLK)], res_v.at[b], load_sem.at[0]
        ).start()
    load_w = pltpu.make_async_copy(local_factor.at[0], w_v, load_sem.at[1])
    load_v = pltpu.make_async_copy(coarse_factor, v_v, load_sem.at[2])
    load_w.start()
    load_v.start()

    barrier = pltpu.get_barrier_semaphore()

    def greet_plane(d, carry):
        pl.semaphore_signal(
            barrier, inc=1, device_id=(grp, lax.rem(me + d, n_sub)), device_id_type=MESH
        )
        return carry

    def greet_column(d, carry):
        pl.semaphore_signal(
            barrier, inc=1, device_id=(lax.rem(grp + d, n_grp), me), device_id_type=MESH
        )
        return carry

    lax.fori_loop(1, n_sub, greet_plane, 0)
    lax.fori_loop(1, n_grp, greet_column, 0)

    place = (
        lax.broadcasted_iota(jnp.int32, (8, BLK), 0) * BLK
        + lax.broadcasted_iota(jnp.int32, (8, BLK), 1)
    )
    mark = jnp.zeros((8, BLK), F32)
    for b in range(own):
        mark = jnp.where(place == q * own + b, (aggregate[b] + 1).astype(F32), mark)
    wait_all(res_v, load_sem.at[0])
    for r in range(rows):
        for b in range(own):
            gathered[q, r * own + b : r * own + b + 1, :] = res_v[
                b, pl.ds(grp * rows + r, 1), :
            ]
    gathered[q, rows * own : rows * own + 8, :] = mark
    pl.semaphore_wait(barrier, n_sub - 1 + n_grp - 1)

    def send_gather(d, carry):
        target = lax.rem(q + d, nq) * 2 + core
        pltpu.make_async_remote_copy(
            src_ref=gathered.at[q], dst_ref=gathered.at[q],
            send_sem=gather_send, recv_sem=gather_recv,
            device_id=(grp, target), device_id_type=MESH,
        ).start()
        return carry

    lax.fori_loop(1, nq, send_gather, 0)

    load_w.wait()
    width = own * BLK
    inner = lax.dot_general(
        jnp.concatenate([res_v[b].astype(BF16) for b in range(own)], axis=1),
        w_v[:, :width], NT, preferred_element_type=F32,
    )
    table_rows = -(-n_sub * margins // BLK)

    def fill_table(s, table):
        for k in range(margins):
            table = jnp.where(place == s * margins + k, margin[s, k], table)
        return table

    table = lax.fori_loop(0, n_sub, fill_table, jnp.full((8, BLK), -1, jnp.int32))
    own_ids = lax.broadcasted_iota(jnp.int32, (own, BLK), 0) + me * own
    owner_hot = jnp.concatenate(
        [
            (jnp.broadcast_to(table[i : i + 1, :], (own, BLK)) == own_ids).astype(F32)
            for i in range(table_rows)
        ],
        axis=1,
    ).astype(BF16)

    wait_all(gathered.at[pl.ds(0, nq - 1)], gather_recv)

    def pick(sub_index, target):
        for k in range(margins):
            block = margin[sub_index, k]
            owner = lax.div(block, own)
            slot = lax.div(owner, 2)
            at = block - owner * own
            for r in range(rows):
                target[r : r + 1, k * BLK : (k + 1) * BLK] = gathered[
                    slot, pl.ds(at + r * own, 1), :
                ]

    pick(pair, pick_out)
    pair_pick = pltpu.make_async_remote_copy(
        src_ref=pick_out, dst_ref=pick_in, send_sem=pair_send.at[0], recv_sem=pair_recv.at[0],
        device_id=(grp, pair), device_id_type=MESH,
    )
    pair_pick.start()
    pick(me, halo.at[grp])

    marks = gathered[0, rows * own : rows * own + 8, :]
    for i in range(1, nq):
        marks = marks + gathered[i, rows * own : rows * own + 8, :]
    depth = nq * own
    tiles = -(-depth // BLK)
    coarse_ids = (lax.broadcasted_iota(jnp.int32, (ncb, BLK), 0) + 1).astype(F32)

    def hot_of(m):
        return jnp.concatenate(
            [
                (jnp.broadcast_to(m[i : i + 1, :], (ncb, BLK)) == coarse_ids).astype(F32)
                for i in range(tiles)
            ],
            axis=1,
        )

    hot = hot_of(marks)
    values = jnp.concatenate(
        [gathered[:, r * own : (r + 1) * own, :].reshape(depth, BLK) for r in range(rows)], axis=1
    )
    part_sums = split_dot(hot[:, :depth].astype(BF16), values)
    sums_out[:ncb, :] = part_sums
    sums_out[ncb:, :BLK] = marks
    sums_out[ncb:, BLK:] = marks
    pair_sums = pltpu.make_async_remote_copy(
        src_ref=sums_out, dst_ref=sums_in, send_sem=pair_send.at[1], recv_sem=pair_recv.at[1],
        device_id=(grp, pair), device_id_type=MESH,
    )
    pair_sums.start()

    pair_pick.wait_recv()
    for k in range(margins):
        owner = lax.div(margin[me, k], own)
        mine = lax.rem(owner, 2) == core
        cols = slice(k * BLK, (k + 1) * BLK)
        halo[grp, :, cols] = jnp.where(mine, halo[grp, :, cols], pick_in[:, cols])

    def column_copy(src, dst, send, recv, d):
        target = lax.rem(grp + d, n_grp)
        return pltpu.make_async_remote_copy(
            src_ref=src(target), dst_ref=dst.at[grp], send_sem=send, recv_sem=recv,
            device_id=(target, me), device_id_type=MESH,
        )

    def send_halo(d, carry):
        column_copy(lambda t: halo.at[grp], halo, halo_send, halo_recv, d).start()
        return carry

    lax.fori_loop(1, n_grp, send_halo, 0)

    pair_sums.wait_recv()
    count = jnp.sum(hot, axis=1, keepdims=True) + jnp.sum(
        hot_of(sums_in[ncb:, :BLK]), axis=1, keepdims=True
    )
    coarse = (part_sums + sums_in[:ncb, :]) / jnp.maximum(count, 1.0)
    for j in range(ncb):
        for r in range(rows):
            c_rows[r : r + 1, j * BLK : (j + 1) * BLK] = coarse[
                j : j + 1, r * BLK : (r + 1) * BLK
            ]
    load_v.wait()
    inner_c = lax.dot_general(
        c_rows[...].astype(BF16), v_v[...], NT, preferred_element_type=F32
    ).astype(BF16)
    e_mine = jnp.dot(inner_c, v_v[...], preferred_element_type=F32)
    for j in range(ncb):
        e_part[j] = e_mine[:, j * BLK : (j + 1) * BLK]

    def send_e_part(d, carry):
        target = lax.rem(me + d, n_sub)
        pltpu.make_async_remote_copy(
            src_ref=e_part.at[pl.ds(target * per, per)], dst_ref=e_recv.at[me],
            send_sem=es_send, recv_sem=es_recv,
            device_id=(grp, target), device_id_type=MESH,
        ).start()
        return carry

    lax.fori_loop(1, n_sub, send_e_part, 0)

    wait_all(halo.at[pl.ds(0, n_grp - 1)], halo_recv)
    halo_rhs = jnp.concatenate([halo[i] for i in range(n_grp)], axis=0).astype(BF16)
    inner = inner + lax.dot_general(
        halo_rhs, w_v[:, width:], NT, preferred_element_type=F32
    )
    inner = inner.astype(BF16)
    sol = jnp.dot(inner, w_v[:, width:], preferred_element_type=F32)
    for i in range(n_grp):
        part_h[i] = sol[i * rows : (i + 1) * rows, :]

    def send_h(d, carry):
        column_copy(lambda t: part_h.at[t], recv_h, h_send, h_recv, d).start()
        return carry

    lax.fori_loop(1, n_grp, send_h, 0)
    sol = jnp.dot(inner, w_v[:, :width], preferred_element_type=F32)
    for i in range(n_grp):
        part_o[i] = sol[i * rows : (i + 1) * rows, :]

    def send_o(d, carry):
        column_copy(lambda t: part_o.at[t], recv_o, o_send, o_recv, d).start()
        return carry

    lax.fori_loop(1, n_grp, send_o, 0)

    wait_all(e_recv.at[pl.ds(0, n_sub - 1)], es_recv)
    e_recv[me] = e_part[pl.ds(me * per, per)]
    e_full[pl.ds(me * per, per)] = jnp.sum(e_recv[...], axis=0)

    def send_e(d, carry):
        target = lax.rem(me + d, n_sub)
        pltpu.make_async_remote_copy(
            src_ref=e_full.at[pl.ds(me * per, per)], dst_ref=e_full.at[pl.ds(me * per, per)],
            send_sem=ea_send, recv_sem=ea_recv,
            device_id=(grp, target), device_id_type=MESH,
        ).start()
        return carry

    lax.fori_loop(1, n_sub, send_e, 0)

    wait_all(recv_h.at[pl.ds(0, n_grp - 1)], h_recv)
    recv_h[grp] = part_h[grp]
    total = jnp.sum(recv_h[...], axis=0)
    for k in range(margins):
        for r in range(rows):
            back[me, k : k + 1, r * BLK : (r + 1) * BLK] = total[
                r : r + 1, k * BLK : (k + 1) * BLK
            ]

    def send_back(d, carry):
        target = lax.rem(me + d, n_sub)
        pltpu.make_async_remote_copy(
            src_ref=back.at[me], dst_ref=back.at[me], send_sem=back_send, recv_sem=back_recv,
            device_id=(grp, target), device_id_type=MESH,
        ).start()
        return carry

    lax.fori_loop(1, n_sub, send_back, 0)

    wait_all(recv_o.at[pl.ds(0, n_grp - 1)], o_recv)
    recv_o[grp] = part_o[grp]
    total = jnp.sum(recv_o[...], axis=0)
    wait_all(e_full.at[pl.ds(0, ncb - per)], ea_recv)
    for b in range(own):
        both = e_full[aggregate[b]] + total[:, b * BLK : (b + 1) * BLK]
        for r in range(rows):
            acc[r, b : b + 1, :] = both[r : r + 1, :]

    wait_all(back.at[pl.ds(0, n_sub - 1)], back_recv)
    returned = split_dot(owner_hot[:, : n_sub * margins], back[...].reshape(n_sub * margins, rows * BLK))
    for r in range(rows):
        out[r] = acc[r] + returned[:, r * BLK : (r + 1) * BLK]

    wait_all(gathered.at[pl.ds(0, nq - 1)], gather_send)
    pair_pick.wait_send()
    pair_sums.wait_send()
    wait_all(halo.at[pl.ds(0, n_grp - 1)], halo_send)
    wait_all(recv_h.at[pl.ds(0, n_grp - 1)], h_send)
    wait_all(recv_o.at[pl.ds(0, n_grp - 1)], o_send)
    wait_all(e_recv.at[pl.ds(0, n_sub - 1)], es_send)
    wait_all(e_full.at[pl.ds(0, ncb - per)], ea_send)
    wait_all(back.at[pl.ds(0, n_sub - 1)], back_send)


def on_device(residual, margin, aggregate, local_factor, coarse_factor):
    n_sub = lax.axis_size("sub")
    n_grp = lax.axis_size("grp")
    rhs, own_width = residual.shape
    own = own_width // BLK
    margins = margin.shape[1]
    inner = local_factor.shape[1]
    nc = coarse_factor.shape[1]
    ncb = nc // BLK
    rows = rhs // n_grp
    nq = n_sub // 2
    hw = margins * BLK
    sizes = (n_sub, n_grp, own, margins, ncb)
    vm = pltpu.VMEM
    sem = pltpu.SemaphoreType.DMA
    result = pl.pallas_call(
        functools.partial(kernel, sizes),
        out_shape=jax.ShapeDtypeStruct((rows, own, BLK), F32),
        in_specs=[
            pl.BlockSpec(memory_space=pltpu.SMEM),
            pl.BlockSpec(memory_space=pltpu.SMEM),
            pl.BlockSpec(memory_space=pl.ANY),
            pl.BlockSpec(memory_space=pl.ANY),
            pl.BlockSpec(memory_space=pl.ANY),
        ],
        out_specs=pl.BlockSpec(memory_space=pltpu.VMEM),
        scratch_shapes=[
            vm((own, rhs, BLK), F32),
            vm((inner, own_width + hw), BF16),
            vm(coarse_factor.shape, BF16),
            vm((nq, rows * own + 8, BLK), F32),
            vm((rows, hw), F32),
            vm((rows, hw), F32),
            vm((ncb + 8, rows * BLK), F32),
            vm((ncb + 8, rows * BLK), F32),
            vm((n_grp, rows, hw), F32),
            vm((rows, nc), F32),
            vm((n_grp, rows, hw), F32),
            vm((n_grp, rows, hw), F32),
            vm((n_grp, rows, own_width), F32),
            vm((n_grp, rows, own_width), F32),
            vm((n_sub, margins, rows * BLK), F32),
            vm((ncb, rows, BLK), F32),
            vm((n_sub, ncb // n_sub, rows, BLK), F32),
            vm((ncb, rows, BLK), F32),
            vm((rows, own, BLK), F32),
            sem((3,)), sem, sem, sem((2,)), sem((2,)), sem, sem,
            sem, sem, sem, sem, sem, sem, sem, sem, sem, sem,
        ],
        compiler_params=pltpu.CompilerParams(collective_id=0, has_side_effects=True),
    )(margin, aggregate, residual, local_factor, coarse_factor)
    return result.reshape(rows, own_width)


def solution(mesh):
    placed = (P(None, "sub"), P(), P("sub"), P("sub", "grp", None), P("sub", None))
    return jax.shard_map(
        on_device, mesh=mesh, in_specs=placed, out_specs=P("grp", "sub"), check_vma=False
    )
```

time: 460 us -> 43.4 us (0.09)
  waiting for transfers between devices: 352 us -> 0 us
  blocking collectives: 65.2 us -> 0 us
  Pallas kernels: 0 us -> 40.4 us
  matrix products: 21.3 us -> 0 us
  between operations: 13.9 us -> 0.01 us
    psum x2 -> x0, waiting for transfers between devices: 155 us -> none  [the longest x1 112 us: on_device(): coarse_sol = lax.psum(coarse_part, 'sub')]
    reduce_scatter x1 -> x0, waiting for transfers between devices: 81.8 us -> none  [on_device(): returned = lax.psum_scatter(spread, 'sub', scatter_dimension=1, tiled=True)]
    psum x1 -> x0, blocking collectives: 65.2 us -> none  [on_device(): sums, counts = lax.psum((sums_part, jnp.sum(member, axis=0)), 'sub')]
    unnamed x6 -> x0, waiting for transfers between devices: 60 us -> none
    all_gather x1 -> x0, waiting for transfers between devices: 55 us -> none  [on_device(): whole = lax.all_gather(blocks, 'sub', axis=1, tiled=True)]
    pallas_call x0 -> x1, Pallas kernels: none -> 40.4 us  [on_device(): pl.pallas_call(functools.partial(kernel, sizes), out_shape=jax.ShapeDtype...]
    dot_general x6 -> x0, matrix products: 21.3 us -> none  [the longest x1 6.35 us: on_device(): jnp.dot(inner_coarse, coarse_factor, preferred_element_type=jnp.float32)]
  transfers between devices with their start and end apart: 5 -> 0, of which waited for: 5 -> 0; matrix products, arithmetic and copies ran while one was open for 3% -> 0% of each run, Pallas kernels for 0% -> 0%
where the time goes in v1:
time: 43.4 us; the launch traced here: 43.1 us
  Pallas kernels  40.4 us (93%)
  local copies, waits for them, and re-layouts  2.72 us (6%)
    pallas_call x1, Pallas kernels, on_device(): pl.pallas_call(functools.partial(kernel, sizes), out_shape=jax.ShapeDtype...  40.4 us
    unnamed x2, local copies, waits for them, and re-layouts  2.72 us

profile of v1, /device:TPU:1, one launch (start us, length us, event | category | flops | bytes accessed | tf_op | source)
XLA Modules:
  0.0 43.1 jit_solution(15151007182780459982)
XLA Ops:
  0.0 1.4 %copy.6.margin = s32[32,8]{1,0:T(8,128)} copy(s32[32,8]{0,1:T(8,128)} %param.6) | data formatting | bytes 2048 | tf_op args[1]
  1.4 40.4 %shard_map.55 = f32[2,24,128]{2,1,0:T(8,128)} custom-call(s32[32,8]{1,0:T(8,128)} %copy.6.margin, s32[24]{0:T(128)} %aggregate.1, f32[16,3072]{1,0:T(8,128)} %residual.1, bf16[1,512,4096]{2,1,0:T(8,128)(2,1)} %local_factor.1, bf16[256,8192]{1,0:T(8,128)(2,1)} %coarse_factor.1), custom_call_target="tpu_custom_call" | custom-call | tf_op jit(solution)/shard_map/pallas_call | solution.py:323
  41.8 1.4 %copy.9 = f32[1,2,24,128]{3,1,2,0:T(2,128)} copy(f32[1,2,24,128]{3,2,1,0:T(8,128)} %bitcast.4) | data formatting | bytes 49152

commit v2 on v0

v2 whole, which is shorter than its diff:
```python
import functools

import jax
import jax.numpy as jnp
from jax import lax
from jax.experimental import pallas as pl
from jax.experimental.pallas import tpu as pltpu
from jax.sharding import PartitionSpec as P

BLK = 128
F32 = jnp.float32
BF16 = jnp.bfloat16
MESH = pl.DeviceIdType.MESH
NT = (((1,), (1,)), ((), ()))
TN = (((0,), (0,)), ((), ()))


def split(values):
    high = values.astype(BF16)
    return high, (values - high.astype(F32)).astype(BF16)


def split_dot(onehot, values):
    high, low = split(values)
    return jnp.dot(onehot, high, preferred_element_type=F32) + jnp.dot(
        onehot, low, preferred_element_type=F32
    )


def wait_all(ref, sem):
    pltpu.make_async_copy(ref, ref, sem).wait()


def kernel(
    sizes,
    margin, aggregate, residual, local_factor, coarse_factor,
    out,
    res_v, w_v, v_v, mine, pick_out, pick_in, c_out, c_in, c_full, halo, inner_v,
    part_h, recv_h, part_o, recv_o, back, e_part, e_recv, e_full, acc,
    load_sem, pick_send, pick_recv, cs_send, cs_recv, ca_send, ca_recv, halo_send, halo_recv,
    h_send, h_recv, o_send, o_recv, back_send, back_recv, es_send, es_recv, ea_send, ea_recv,
):
    n_sub, n_grp, own, margins, ncb = sizes
    rows = 2
    per = ncb // n_sub
    me = lax.axis_index("sub")
    grp = lax.axis_index("grp")

    for b in range(own):
        pltpu.make_async_copy(
            residual.at[:, pl.ds(b * BLK, BLK)],
            res_v.at[pl.ds(b * rows * n_grp, rows * n_grp)],
            load_sem.at[0],
        ).start()
    load_w = pltpu.make_async_copy(local_factor.at[0], w_v, load_sem.at[1])
    load_v = pltpu.make_async_copy(coarse_factor, v_v, load_sem.at[2])
    load_w.start()
    load_v.start()

    barrier = pltpu.get_barrier_semaphore()

    def plane(d):
        return (grp, lax.rem(me + d, n_sub))

    def column(d):
        return (lax.rem(grp + d, n_grp), me)

    for d in range(1, n_sub):
        pl.semaphore_signal(barrier, inc=1, device_id=plane(d), device_id_type=MESH)
    for d in range(1, n_grp):
        pl.semaphore_signal(barrier, inc=1, device_id=column(d), device_id_type=MESH)

    def to_plane(src, dst, send, recv):
        for d in range(1, n_sub):
            target = plane(d)
            pltpu.make_async_remote_copy(
                src_ref=src(target[1]), dst_ref=dst, send_sem=send, recv_sem=recv,
                device_id=target, device_id_type=MESH,
            ).start()

    def to_column(src, dst, send, recv):
        for d in range(1, n_grp):
            target = column(d)
            pltpu.make_async_remote_copy(
                src_ref=src(target[0]), dst_ref=dst, send_sem=send, recv_sem=recv,
                device_id=target, device_id_type=MESH,
            ).start()

    place = (
        lax.broadcasted_iota(jnp.int32, (8, BLK), 0) * BLK
        + lax.broadcasted_iota(jnp.int32, (8, BLK), 1)
    )
    slots = n_sub * margins

    def fill_table(s, table):
        for k in range(margins):
            table = jnp.where(place == s * margins + k, margin[k, s], table)
        return table

    table = lax.fori_loop(0, n_sub, fill_table, jnp.full((8, BLK), -1, jnp.int32))
    own_ids = lax.broadcasted_iota(jnp.int32, (own, BLK), 0) + me * own
    owner_hot = jnp.concatenate(
        [
            (jnp.broadcast_to(table[i : i + 1, :], (own, BLK)) == own_ids).astype(F32)
            for i in range(-(-slots // BLK))
        ],
        axis=1,
    )[:, :slots]
    mark = jnp.full((8, BLK), -1, jnp.int32)
    for b in range(own):
        mark = jnp.where(place == b, aggregate[b], mark)
    coarse_hot = (
        jnp.broadcast_to(mark[0:1, :], (ncb, BLK))
        == lax.broadcasted_iota(jnp.int32, (ncb, BLK), 0)
    ).astype(F32)

    wait_all(res_v, load_sem.at[0])
    for b in range(own):
        for r in range(rows):
            mine[r * own + b : r * own + b + 1, :] = res_v[
                pl.ds(b * rows * n_grp + grp * rows + r, 1), :
            ]
    blocks = jnp.concatenate([mine[r * own : (r + 1) * own, :] for r in range(rows)], axis=1)
    high, low = split(blocks)
    picked = lax.dot_general(owner_hot.astype(BF16), high, TN, preferred_element_type=F32)
    for r in range(rows):
        pick_out[:, r * margins : (r + 1) * margins, :] = picked[
            :, r * BLK : (r + 1) * BLK
        ].reshape(n_sub, margins, BLK)
    hot = coarse_hot[:, :own].astype(BF16)
    sums = jnp.dot(hot, high, preferred_element_type=F32) + jnp.dot(
        hot, low, preferred_element_type=F32
    )
    count = jnp.broadcast_to(jnp.sum(coarse_hot, axis=1, keepdims=True), (ncb, BLK))
    sums = jnp.concatenate([sums, count], axis=1)
    for t in range(n_sub):
        c_out[t] = sums[t * per : (t + 1) * per, :]

    pl.semaphore_wait(barrier, n_sub - 1 + n_grp - 1)
    to_plane(lambda t: pick_out.at[t], pick_in.at[me], pick_send, pick_recv)
    to_plane(lambda t: c_out.at[t], c_in.at[me], cs_send, cs_recv)

    load_w.wait()
    width = own * BLK
    deep = rows * n_grp
    inner = lax.dot_general(
        jnp.concatenate(
            [res_v[b * deep : (b + 1) * deep, :].astype(BF16) for b in range(own)], axis=1
        ),
        w_v[:, :width], NT, preferred_element_type=F32,
    )
    inner_tiles = inner.shape[1] // BLK
    for i in range(inner_tiles):
        inner_v[i * deep : (i + 1) * deep, :] = inner[:, i * BLK : (i + 1) * BLK]

    wait_all(pick_in.at[pl.ds(0, n_sub - 1)], pick_recv)
    hr = rows * margins
    pick_in[me] = jnp.zeros((hr, BLK), F32)
    halo[pl.ds(grp * hr, hr)] = jnp.sum(pick_in[...], axis=0)
    mine_halo = halo.at[pl.ds(grp * hr, hr)]
    to_column(lambda t: mine_halo, mine_halo, halo_send, halo_recv)

    wait_all(c_in.at[pl.ds(0, n_sub - 1)], cs_recv)
    c_in[me] = c_out[me]
    sums = jnp.sum(c_in[...], axis=0)
    coarse = sums[:, : rows * BLK] / jnp.maximum(
        jnp.concatenate([sums[:, rows * BLK :]] * rows, axis=1), 1.0
    )
    for i in range(per):
        for r in range(rows):
            c_full[me * per + i, r : r + 1, :] = coarse[i : i + 1, r * BLK : (r + 1) * BLK]
    mine_c = c_full.at[pl.ds(me * per, per)]
    to_plane(lambda t: mine_c, mine_c, ca_send, ca_recv)

    wait_all(halo.at[pl.ds(0, (n_grp - 1) * hr)], halo_recv)
    halo_rhs = jnp.concatenate(
        [
            jnp.concatenate(
                [
                    halo[pl.ds(r * margins + k, n_grp, stride=hr), :]
                    for k in range(margins)
                ],
                axis=1,
            )
            for r in range(rows)
        ],
        axis=0,
    ).astype(BF16)
    inner = jnp.concatenate(
        [
            jnp.concatenate(
                [
                    inner_v[pl.ds(i * deep + r, n_grp, stride=rows), :]
                    for i in range(inner_tiles)
                ],
                axis=1,
            )
            for r in range(rows)
        ],
        axis=0,
    )
    inner = inner + lax.dot_general(halo_rhs, w_v[:, width:], NT, preferred_element_type=F32)
    inner = inner.astype(BF16)

    def scatter_rows(sol, dst, blocks_each):
        for r in range(rows):
            for k in range(blocks_each):
                dst[pl.ds(r * blocks_each + k, n_grp, stride=rows * blocks_each), :] = sol[
                    r * n_grp : (r + 1) * n_grp, k * BLK : (k + 1) * BLK
                ]

    scatter_rows(jnp.dot(inner, w_v[:, width:], preferred_element_type=F32), part_h, margins)
    to_column(
        lambda t: part_h.at[pl.ds(t * hr, hr)], recv_h.at[pl.ds(grp * hr, hr)], h_send, h_recv
    )

    wait_all(c_full.at[pl.ds(0, ncb - per)], ca_recv)
    load_v.wait()
    c_rows = jnp.concatenate([c_full[j] for j in range(ncb)], axis=1).astype(BF16)
    inner_c = lax.dot_general(c_rows, v_v[...], NT, preferred_element_type=F32).astype(BF16)
    e_mine = jnp.dot(inner_c, v_v[...], preferred_element_type=F32)
    for j in range(ncb):
        e_part[j] = e_mine[:, j * BLK : (j + 1) * BLK]
    to_plane(lambda t: e_part.at[pl.ds(t * per, per)], e_recv.at[me], es_send, es_recv)

    scatter_rows(jnp.dot(inner, w_v[:, :width], preferred_element_type=F32), part_o, own)
    orr = rows * own
    to_column(
        lambda t: part_o.at[pl.ds(t * orr, orr)], recv_o.at[pl.ds(grp * orr, orr)], o_send, o_recv
    )

    wait_all(recv_h.at[pl.ds(0, (n_grp - 1) * hr)], h_recv)
    recv_h[pl.ds(grp * hr, hr)] = part_h[pl.ds(grp * hr, hr)]
    back[me] = jnp.sum(recv_h[...].reshape(n_grp, hr, BLK), axis=0)
    to_plane(lambda t: back.at[me], back.at[me], back_send, back_recv)

    wait_all(e_recv.at[pl.ds(0, n_sub - 1)], es_recv)
    e_recv[me] = e_part[pl.ds(me * per, per)]
    e_full[pl.ds(me * per, per)] = jnp.sum(e_recv[...], axis=0)
    mine_e = e_full.at[pl.ds(me * per, per)]
    to_plane(lambda t: mine_e, mine_e, ea_send, ea_recv)

    wait_all(recv_o.at[pl.ds(0, (n_grp - 1) * orr)], o_recv)
    recv_o[pl.ds(grp * orr, orr)] = part_o[pl.ds(grp * orr, orr)]
    total = jnp.sum(recv_o[...].reshape(n_grp, orr, BLK), axis=0)
    wait_all(e_full.at[pl.ds(0, ncb - per)], ea_recv)
    for b in range(own):
        acc[b * rows : (b + 1) * rows, :] = e_full[aggregate[b]]
    for r in range(rows):
        acc[pl.ds(r, own, stride=rows), :] = (
            acc[pl.ds(r, own, stride=rows), :] + total[r * own : (r + 1) * own, :]
        )

    wait_all(back.at[pl.ds(0, n_sub - 1)], back_recv)
    values = jnp.concatenate(
        [
            back[:, r * margins : (r + 1) * margins, :].reshape(slots, BLK)
            for r in range(rows)
        ],
        axis=1,
    )
    returned = split_dot(owner_hot.astype(BF16), values)
    for r in range(rows):
        out[pl.ds(r, own, stride=rows), :] = (
            acc[pl.ds(r, own, stride=rows), :] + returned[:, r * BLK : (r + 1) * BLK]
        )

    wait_all(pick_in.at[pl.ds(0, n_sub - 1)], pick_send)
    wait_all(c_in.at[pl.ds(0, n_sub - 1)], cs_send)
    wait_all(halo.at[pl.ds(0, (n_grp - 1) * hr)], halo_send)
    wait_all(c_full.at[pl.ds(0, ncb - per)], ca_send)
    wait_all(recv_h.at[pl.ds(0, (n_grp - 1) * hr)], h_send)
    wait_all(recv_o.at[pl.ds(0, (n_grp - 1) * orr)], o_send)
    wait_all(e_recv.at[pl.ds(0, n_sub - 1)], es_send)
    wait_all(e_full.at[pl.ds(0, ncb - per)], ea_send)
    wait_all(back.at[pl.ds(0, n_sub - 1)], back_send)


def on_device(residual, margin, aggregate, local_factor, coarse_factor):
    n_sub = lax.axis_size("sub")
    n_grp = lax.axis_size("grp")
    rhs, own_width = residual.shape
    own = own_width // BLK
    margins = margin.shape[1]
    inner = local_factor.shape[1]
    ncb = coarse_factor.shape[1] // BLK
    rows = rhs // n_grp
    per = ncb // n_sub
    sizes = (n_sub, n_grp, own, margins, ncb)
    vm = pltpu.VMEM
    sem = pltpu.SemaphoreType.DMA
    result = pl.pallas_call(
        functools.partial(kernel, sizes),
        out_shape=jax.ShapeDtypeStruct((rows * own, BLK), F32),
        in_specs=[
            pl.BlockSpec(memory_space=pltpu.SMEM),
            pl.BlockSpec(memory_space=pltpu.SMEM),
            pl.BlockSpec(memory_space=pl.ANY),
            pl.BlockSpec(memory_space=pl.ANY),
            pl.BlockSpec(memory_space=pl.ANY),
        ],
        out_specs=pl.BlockSpec(memory_space=pltpu.VMEM),
        scratch_shapes=[
            vm((own * rhs, BLK), F32),
            vm((inner, own_width + margins * BLK), BF16),
            vm(coarse_factor.shape, BF16),
            vm((rows * own, BLK), F32),
            vm((n_sub, rows * margins, BLK), F32),
            vm((n_sub, rows * margins, BLK), F32),
            vm((n_sub, per, (rows + 1) * BLK), F32),
            vm((n_sub, per, (rows + 1) * BLK), F32),
            vm((ncb, rows, BLK), F32),
            vm((n_grp * rows * margins, BLK), F32),
            vm((rhs * inner // BLK, BLK), F32),
            vm((n_grp * rows * margins, BLK), F32),
            vm((n_grp * rows * margins, BLK), F32),
            vm((n_grp * rows * own, BLK), F32),
            vm((n_grp * rows * own, BLK), F32),
            vm((n_sub, rows * margins, BLK), F32),
            vm((ncb, rows, BLK), F32),
            vm((n_sub, per, rows, BLK), F32),
            vm((ncb, rows, BLK), F32),
            vm((rows * own, BLK), F32),
            sem((3,)),
        ] + [sem] * 18,
        compiler_params=pltpu.CompilerParams(collective_id=0, has_side_effects=True),
    )(margin.T, aggregate, residual, local_factor, coarse_factor)
    return result.reshape(own, rows, BLK).transpose(1, 0, 2).reshape(rows, own_width)


def solution(mesh):
    placed = (P(None, "sub"), P(), P("sub"), P("sub", "grp", None), P("sub", None))
    return jax.shard_map(
        on_device, mesh=mesh, in_specs=placed, out_specs=P("grp", "sub"), check_vma=False
    )
```

time: 460 us -> 39.8 us (0.09)
  waiting for transfers between devices: 352 us -> 0 us
  blocking collectives: 65.2 us -> 0 us
  Pallas kernels: 0 us -> 38.3 us
  matrix products: 21.3 us -> 0 us
  between operations: 13.9 us -> 0.01 us
    psum x2 -> x0, waiting for transfers between devices: 155 us -> none  [the longest x1 112 us: on_device(): coarse_sol = lax.psum(coarse_part, 'sub')]
    reduce_scatter x1 -> x0, waiting for transfers between devices: 81.8 us -> none  [on_device(): returned = lax.psum_scatter(spread, 'sub', scatter_dimension=1, tiled=True)]
    psum x1 -> x0, blocking collectives: 65.2 us -> none  [on_device(): sums, counts = lax.psum((sums_part, jnp.sum(member, axis=0)), 'sub')]
    unnamed x6 -> x0, waiting for transfers between devices: 60 us -> none
    all_gather x1 -> x0, waiting for transfers between devices: 55 us -> none  [on_device(): whole = lax.all_gather(blocks, 'sub', axis=1, tiled=True)]
    pallas_call x0 -> x1, Pallas kernels: none -> 38.3 us  [on_device(): pl.pallas_call(functools.partial(kernel, sizes), out_shape=jax.ShapeDtype...]
    dot_general x6 -> x0, matrix products: 21.3 us -> none  [the longest x1 6.35 us: on_device(): jnp.dot(inner_coarse, coarse_factor, preferred_element_type=jnp.float32)]
  transfers between devices with their start and end apart: 5 -> 0, of which waited for: 5 -> 0; matrix products, arithmetic and copies ran while one was open for 3% -> 0% of each run, Pallas kernels for 0% -> 0%
where the time goes in v2:
time: 39.8 us; the launch traced here: 39.6 us
  Pallas kernels  38.3 us (96%)
  local copies, waits for them, and re-layouts  1.35 us (3%)
    pallas_call x1, Pallas kernels, on_device(): pl.pallas_call(functools.partial(kernel, sizes), out_shape=jax.ShapeDtype...  38.3 us
    unnamed x1, local copies, waits for them, and re-layouts  1.35 us

profile of v2, /device:TPU:1, one launch (start us, length us, event | category | flops | bytes accessed | tf_op | source)
XLA Modules:
  0.0 39.6 jit_solution(17918777496540640652)
XLA Ops:
  0.0 38.3 %shard_map.55 = f32[48,128]{1,0:T(8,128)} custom-call(s32[8,32]{1,0:T(8,128)} %bitcast.7, s32[24]{0:T(128)} %aggregate.1, f32[16,3072]{1,0:T(8,128)} %residual.1, bf16[1,512,4096]{2,1,0:T(8,128)(2,1)} %local_factor.1, bf16[256,8192]{1,0:T(8,128)(2,1)} %coarse_factor.1), custom_call_target="tpu_custom_call" | custom-call | tf_op jit(solution)/shard_map/pallas_call | solution.py:292
  38.3 1.3 %copy.8 = f32[2,3072]{1,0:T(2,128)} copy(f32[2,3072]{1,0:T(2,128)} %bitcast.6) | data formatting | bytes 49152

commit v3 on v2

--- a/solution.py
+++ b/solution.py
@@ -35,9 +35,9 @@
     sizes,
     margin, aggregate, residual, local_factor, coarse_factor,
     out,
-    res_v, w_v, v_v, mine, pick_out, pick_in, c_out, c_in, c_full, halo, inner_v,
+    margin_v, agg_v, agg_s, res_v, w_v, v_v, mine, pick_out, pick_in, c_out, c_in, c_full, halo, inner_v,
     part_h, recv_h, part_o, recv_o, back, e_part, e_recv, e_full, acc,
-    load_sem, pick_send, pick_recv, cs_send, cs_recv, ca_send, ca_recv, halo_send, halo_recv,
+    fence, load_sem, pick_send, pick_recv, cs_send, cs_recv, ca_send, ca_recv, halo_send, halo_recv,
     h_send, h_recv, o_send, o_recv, back_send, back_recv, es_send, es_recv, ea_send, ea_recv,
 ):
     n_sub, n_grp, own, margins, ncb = sizes
@@ -46,6 +46,25 @@
     me = lax.axis_index("sub")
     grp = lax.axis_index("grp")
 
+    barrier = pltpu.get_barrier_semaphore()
+
+    def plane(d):
+        return (grp, lax.rem(me + d, n_sub))
+
+    def column(d):
+        return (lax.rem(grp + d, n_grp), me)
+
+    for d in range(1, n_sub):
+        pl.semaphore_signal(barrier, inc=1, device_id=plane(d), device_id_type=MESH)
+    for d in range(1, n_grp):
+        pl.semaphore_signal(barrier, inc=1, device_id=column(d), device_id_type=MESH)
+
+    load_margin = pltpu.make_async_copy(margin, margin_v, load_sem.at[3])
+    load_agg = pltpu.make_async_copy(aggregate, agg_v, load_sem.at[4])
+    load_ids = pltpu.make_async_copy(aggregate, agg_s, load_sem.at[5])
+    load_margin.start()
+    load_agg.start()
+    load_ids.start()
     for b in range(own):
         pltpu.make_async_copy(
             residual.at[:, pl.ds(b * BLK, BLK)],
@@ -57,19 +76,6 @@
     load_w.start()
     load_v.start()
 
-    barrier = pltpu.get_barrier_semaphore()
-
-    def plane(d):
-        return (grp, lax.rem(me + d, n_sub))
-
-    def column(d):
-        return (lax.rem(grp + d, n_grp), me)
-
-    for d in range(1, n_sub):
-        pl.semaphore_signal(barrier, inc=1, device_id=plane(d), device_id_type=MESH)
-    for d in range(1, n_grp):
-        pl.semaphore_signal(barrier, inc=1, device_id=column(d), device_id_type=MESH)
-
     def to_plane(src, dst, send, recv):
         for d in range(1, n_sub):
             target = plane(d)
@@ -86,32 +92,27 @@
                 device_id=target, device_id_type=MESH,
             ).start()
 
-    place = (
-        lax.broadcasted_iota(jnp.int32, (8, BLK), 0) * BLK
-        + lax.broadcasted_iota(jnp.int32, (8, BLK), 1)
-    )
+    def fenced():
+        pl.semaphore_signal(fence, 1)
+        pl.semaphore_wait(fence, 1)
+
     slots = n_sub * margins
-
-    def fill_table(s, table):
-        for k in range(margins):
-            table = jnp.where(place == s * margins + k, margin[k, s], table)
-        return table
-
-    table = lax.fori_loop(0, n_sub, fill_table, jnp.full((8, BLK), -1, jnp.int32))
+    each = BLK // n_sub
+    lane = lax.broadcasted_iota(jnp.int32, (1, BLK), 1)
     own_ids = lax.broadcasted_iota(jnp.int32, (own, BLK), 0) + me * own
-    owner_hot = jnp.concatenate(
-        [
-            (jnp.broadcast_to(table[i : i + 1, :], (own, BLK)) == own_ids).astype(F32)
-            for i in range(-(-slots // BLK))
-        ],
-        axis=1,
-    )[:, :slots]
-    mark = jnp.full((8, BLK), -1, jnp.int32)
-    for b in range(own):
-        mark = jnp.where(place == b, aggregate[b], mark)
+    load_margin.wait()
+    spread = jnp.concatenate([margin_v[...]] * each, axis=1)
+    tables = []
+    for first in range(0, margins, each):
+        row = jnp.full((1, BLK), -1, jnp.int32)
+        for i in range(min(each, margins - first)):
+            here = jnp.logical_and(lane >= i * n_sub, lane < (i + 1) * n_sub)
+            row = jnp.where(here, spread[first + i : first + i + 1, :], row)
+        tables.append((jnp.broadcast_to(row, (own, BLK)) == own_ids).astype(F32))
+    owner_hot = jnp.concatenate(tables, axis=1)[:, :slots]
+    load_agg.wait()
     coarse_hot = (
-        jnp.broadcast_to(mark[0:1, :], (ncb, BLK))
-        == lax.broadcasted_iota(jnp.int32, (ncb, BLK), 0)
+        jnp.broadcast_to(agg_v[...], (ncb, own)) == lax.broadcasted_iota(jnp.int32, (ncb, own), 0)
     ).astype(F32)
 
     wait_all(res_v, load_sem.at[0])
@@ -123,11 +124,15 @@
     blocks = jnp.concatenate([mine[r * own : (r + 1) * own, :] for r in range(rows)], axis=1)
     high, low = split(blocks)
     picked = lax.dot_general(owner_hot.astype(BF16), high, TN, preferred_element_type=F32)
+    hr = rows * margins
     for r in range(rows):
-        pick_out[:, r * margins : (r + 1) * margins, :] = picked[
-            :, r * BLK : (r + 1) * BLK
-        ].reshape(n_sub, margins, BLK)
-    hot = coarse_hot[:, :own].astype(BF16)
+        for k in range(margins):
+            for t in range(0, n_sub, 8):
+                at = k * n_sub + t
+                pick_out[pl.ds(t * hr + r * margins + k, 8, stride=hr), :] = picked[
+                    at : at + 8, r * BLK : (r + 1) * BLK
+                ]
+    hot = coarse_hot.astype(BF16)
     sums = jnp.dot(hot, high, preferred_element_type=F32) + jnp.dot(
         hot, low, preferred_element_type=F32
     )
@@ -137,7 +142,7 @@
         c_out[t] = sums[t * per : (t + 1) * per, :]
 
     pl.semaphore_wait(barrier, n_sub - 1 + n_grp - 1)
-    to_plane(lambda t: pick_out.at[t], pick_in.at[me], pick_send, pick_recv)
+    to_plane(lambda t: pick_out.at[pl.ds(t * hr, hr)], pick_in.at[me], pick_send, pick_recv)
     to_plane(lambda t: c_out.at[t], c_in.at[me], cs_send, cs_recv)
 
     load_w.wait()
@@ -154,7 +159,6 @@
         inner_v[i * deep : (i + 1) * deep, :] = inner[:, i * BLK : (i + 1) * BLK]
 
     wait_all(pick_in.at[pl.ds(0, n_sub - 1)], pick_recv)
-    hr = rows * margins
     pick_in[me] = jnp.zeros((hr, BLK), F32)
     halo[pl.ds(grp * hr, hr)] = jnp.sum(pick_in[...], axis=0)
     mine_halo = halo.at[pl.ds(grp * hr, hr)]
@@ -201,6 +205,7 @@
     )
     inner = inner + lax.dot_general(halo_rhs, w_v[:, width:], NT, preferred_element_type=F32)
     inner = inner.astype(BF16)
+    fenced()
 
     def scatter_rows(sol, dst, blocks_each):
         for r in range(rows):
@@ -218,6 +223,7 @@
     load_v.wait()
     c_rows = jnp.concatenate([c_full[j] for j in range(ncb)], axis=1).astype(BF16)
     inner_c = lax.dot_general(c_rows, v_v[...], NT, preferred_element_type=F32).astype(BF16)
+    fenced()
     e_mine = jnp.dot(inner_c, v_v[...], preferred_element_type=F32)
     for j in range(ncb):
         e_part[j] = e_mine[:, j * BLK : (j + 1) * BLK]
@@ -231,8 +237,9 @@
 
     wait_all(recv_h.at[pl.ds(0, (n_grp - 1) * hr)], h_recv)
     recv_h[pl.ds(grp * hr, hr)] = part_h[pl.ds(grp * hr, hr)]
-    back[me] = jnp.sum(recv_h[...].reshape(n_grp, hr, BLK), axis=0)
-    to_plane(lambda t: back.at[me], back.at[me], back_send, back_recv)
+    mine_back = back.at[pl.ds(me * hr, hr)]
+    back[pl.ds(me * hr, hr)] = jnp.sum(recv_h[...].reshape(n_grp, hr, BLK), axis=0)
+    to_plane(lambda t: mine_back, mine_back, back_send, back_recv)
 
     wait_all(e_recv.at[pl.ds(0, n_sub - 1)], es_recv)
     e_recv[me] = e_part[pl.ds(me * per, per)]
@@ -244,17 +251,25 @@
     recv_o[pl.ds(grp * orr, orr)] = part_o[pl.ds(grp * orr, orr)]
     total = jnp.sum(recv_o[...].reshape(n_grp, orr, BLK), axis=0)
     wait_all(e_full.at[pl.ds(0, ncb - per)], ea_recv)
+    load_ids.wait()
     for b in range(own):
-        acc[b * rows : (b + 1) * rows, :] = e_full[aggregate[b]]
+        acc[b * rows : (b + 1) * rows, :] = e_full[agg_s[0, b]]
     for r in range(rows):
         acc[pl.ds(r, own, stride=rows), :] = (
             acc[pl.ds(r, own, stride=rows), :] + total[r * own : (r + 1) * own, :]
         )
 
-    wait_all(back.at[pl.ds(0, n_sub - 1)], back_recv)
+    wait_all(back.at[pl.ds(0, (n_sub - 1) * hr)], back_recv)
     values = jnp.concatenate(
         [
-            back[:, r * margins : (r + 1) * margins, :].reshape(slots, BLK)
+            jnp.concatenate(
+                [
+                    back[pl.ds(s * hr + r * margins + k, 8, stride=hr), :]
+                    for k in range(margins)
+                    for s in range(0, n_sub, 8)
+                ],
+                axis=0,
+            )
             for r in range(rows)
         ],
         axis=1,
@@ -273,7 +288,7 @@
     wait_all(recv_o.at[pl.ds(0, (n_grp - 1) * orr)], o_send)
     wait_all(e_recv.at[pl.ds(0, n_sub - 1)], es_send)
     wait_all(e_full.at[pl.ds(0, ncb - per)], ea_send)
-    wait_all(back.at[pl.ds(0, n_sub - 1)], back_send)
+    wait_all(back.at[pl.ds(0, (n_sub - 1) * hr)], back_send)
 
 
 def on_device(residual, margin, aggregate, local_factor, coarse_factor):
@@ -291,21 +306,24 @@
     sem = pltpu.SemaphoreType.DMA
     result = pl.pallas_call(
         functools.partial(kernel, sizes),
-        out_shape=jax.ShapeDtypeStruct((rows * own, BLK), F32),
+        out_shape=pltpu.VMEM((rows * own, BLK), F32),
         in_specs=[
-            pl.BlockSpec(memory_space=pltpu.SMEM),
-            pl.BlockSpec(memory_space=pltpu.SMEM),
+            pl.BlockSpec(memory_space=pl.ANY),
+            pl.BlockSpec(memory_space=pl.ANY),
             pl.BlockSpec(memory_space=pl.ANY),
             pl.BlockSpec(memory_space=pl.ANY),
             pl.BlockSpec(memory_space=pl.ANY),
         ],
         out_specs=pl.BlockSpec(memory_space=pltpu.VMEM),
         scratch_shapes=[
+            vm((margins, n_sub), jnp.int32),
+            vm((1, own), jnp.int32),
+            pltpu.SMEM((1, own), jnp.int32),
             vm((own * rhs, BLK), F32),
             vm((inner, own_width + margins * BLK), BF16),
             vm(coarse_factor.shape, BF16),
             vm((rows * own, BLK), F32),
-            vm((n_sub, rows * margins, BLK), F32),
+            vm((n_sub * rows * margins, BLK), F32),
             vm((n_sub, rows * margins, BLK), F32),
             vm((n_sub, per, (rows + 1) * BLK), F32),
             vm((n_sub, per, (rows + 1) * BLK), F32),
@@ -316,15 +334,16 @@
             vm((n_grp * rows * margins, BLK), F32),
             vm((n_grp * rows * own, BLK), F32),
             vm((n_grp * rows * own, BLK), F32),
-            vm((n_sub, rows * margins, BLK), F32),
+            vm((n_sub * rows * margins, BLK), F32),
             vm((ncb, rows, BLK), F32),
             vm((n_sub, per, rows, BLK), F32),
             vm((ncb, rows, BLK), F32),
             vm((rows * own, BLK), F32),
-            sem((3,)),
+            pltpu.SemaphoreType.REGULAR,
+            sem((6,)),
         ] + [sem] * 18,
         compiler_params=pltpu.CompilerParams(collective_id=0, has_side_effects=True),
-    )(margin.T, aggregate, residual, local_factor, coarse_factor)
+    )(margin.T, aggregate.reshape(1, own), residual, local_factor, coarse_factor)
     return result.reshape(own, rows, BLK).transpose(1, 0, 2).reshape(rows, own_width)
 
 

time: 39.8 us -> 37.7 us (0.947)
  Pallas kernels: 38.3 us -> 37 us
  local copies, waits for them, and re-layouts: 1.35 us -> 0.61 us
    pallas_call x1, Pallas kernels: 38.3 us -> 37 us  [on_device(): pl.pallas_call(functools.partial(kernel, sizes), out_shape=pltpu.VMEM((ro...]
    unnamed x1, local copies, waits for them, and re-layouts: 1.35 us -> 0.61 us
where the time goes in v3:
time: 37.7 us; the launch traced here: 37.6 us
  Pallas kernels  37 us (98%)
  local copies, waits for them, and re-layouts  0.61 us (2%)
    pallas_call x1, Pallas kernels, on_device(): pl.pallas_call(functools.partial(kernel, sizes), out_shape=pltpu.VMEM((ro...  37 us

profile of v3, /device:TPU:1, one launch (start us, length us, event | category | flops | bytes accessed | tf_op | source)
XLA Modules:
  0.0 37.6 jit_solution(13055400149848259952)
XLA Ops:
  0.0 37.0 %shard_map.55 = f32[48,128]{1,0:T(8,128)S(1)} custom-call(s32[8,32]{1,0:T(8,128)} %bitcast.8, s32[1,24]{1,0:T(1,128)} %bitcast.9, f32[16,3072]{1,0:T(8,128)} %residual.1, bf16[1,512,4096]{2,1,0:T(8,128)(2,1)} %local_factor.1, bf16[256,8192]{1,0:T(8,128)(2,1)} %coarse_factor.1), custom_call_target="tpu_custom_call" | custom-call | tf_op jit(solution)/shard_map/pallas_call | solution.py:307
  37.0 0.6 %copy.8 = f32[2,3072]{1,0:T(2,128)} copy(f32[2,3072]{1,0:T(2,128)S(1)} %bitcast.7) | data formatting | bytes 49152

commit v4 on v3

--- a/solution.py
+++ b/solution.py
@@ -48,16 +48,26 @@
 
     barrier = pltpu.get_barrier_semaphore()
 
-    def plane(d):
-        return (grp, lax.rem(me + d, n_sub))
-
-    def column(d):
-        return (lax.rem(grp + d, n_grp), me)
-
-    for d in range(1, n_sub):
-        pl.semaphore_signal(barrier, inc=1, device_id=plane(d), device_id_type=MESH)
-    for d in range(1, n_grp):
-        pl.semaphore_signal(barrier, inc=1, device_id=column(d), device_id_type=MESH)
+    ny = 4
+    nx = n_sub // (2 * ny)
+    x = lax.div(me, 2 * ny)
+    y = lax.rem(lax.div(me, 2), ny)
+    core = lax.rem(me, 2)
+
+    def far(d, n):
+        return min(d, n - d)
+
+    steps = [(dx, dy, dc) for dx in range(nx) for dy in range(ny) for dc in range(2)]
+    steps = sorted(steps[1:], key=lambda t: -far(t[0], nx) - far(t[1], ny))
+    xs = [lax.rem(x + d, nx) * (2 * ny) for d in range(nx)]
+    ys = [lax.rem(y + d, ny) * 2 for d in range(ny)]
+    cores = [core, 1 - core]
+    plane = [(grp, xs[dx] + ys[dy] + cores[dc]) for dx, dy, dc in steps]
+    column = [
+        (lax.rem(grp + d, n_grp), me) for d in sorted(range(1, n_grp), key=lambda d: -far(d, n_grp))
+    ]
+    for target in plane + column:
+        pl.semaphore_signal(barrier, inc=1, device_id=target, device_id_type=MESH)
 
     load_margin = pltpu.make_async_copy(margin, margin_v, load_sem.at[3])
     load_agg = pltpu.make_async_copy(aggregate, agg_v, load_sem.at[4])
@@ -77,16 +87,14 @@
     load_v.start()
 
     def to_plane(src, dst, send, recv):
-        for d in range(1, n_sub):
-            target = plane(d)
+        for target in plane:
             pltpu.make_async_remote_copy(
                 src_ref=src(target[1]), dst_ref=dst, send_sem=send, recv_sem=recv,
                 device_id=target, device_id_type=MESH,
             ).start()
 
     def to_column(src, dst, send, recv):
-        for d in range(1, n_grp):
-            target = column(d)
+        for target in column:
             pltpu.make_async_remote_copy(
                 src_ref=src(target[0]), dst_ref=dst, send_sem=send, recv_sem=recv,
                 device_id=target, device_id_type=MESH,
@@ -222,7 +230,16 @@
     wait_all(c_full.at[pl.ds(0, ncb - per)], ca_recv)
     load_v.wait()
     c_rows = jnp.concatenate([c_full[j] for j in range(ncb)], axis=1).astype(BF16)
-    inner_c = lax.dot_general(c_rows, v_v[...], NT, preferred_element_type=F32).astype(BF16)
+    panel = v_v.shape[0]
+    inner_c = jnp.concatenate(
+        [
+            lax.dot_general(
+                c_rows, v_v[first : first + panel // 2, :], NT, preferred_element_type=F32
+            )
+            for first in (0, panel // 2)
+        ],
+        axis=1,
+    ).astype(BF16)
     fenced()
     e_mine = jnp.dot(inner_c, v_v[...], preferred_element_type=F32)
     for j in range(ncb):

time: 37.7 us -> 34.5 us (0.915)
  Pallas kernels: 37 us -> 33.8 us
    pallas_call x1, Pallas kernels: 37 us -> 33.8 us  [on_device(): pl.pallas_call(functools.partial(kernel, sizes), out_shape=pltpu.VMEM((ro...]
where the time goes in v4:
time: 34.5 us; the launch traced here: 34.4 us
  Pallas kernels  33.8 us (98%)
  local copies, waits for them, and re-layouts  0.61 us (2%)
    pallas_call x1, Pallas kernels, on_device(): pl.pallas_call(functools.partial(kernel, sizes), out_shape=pltpu.VMEM((ro...  33.8 us

profile of v4, /device:TPU:1, one launch (start us, length us, event | category | flops | bytes accessed | tf_op | source)
XLA Modules:
  0.0 34.4 jit_solution(13902048078818757692)
XLA Ops:
  0.0 33.8 %shard_map.55 = f32[48,128]{1,0:T(8,128)S(1)} custom-call(s32[8,32]{1,0:T(8,128)} %bitcast.8, s32[1,24]{1,0:T(1,128)} %bitcast.9, f32[16,3072]{1,0:T(8,128)} %residual.1, bf16[1,512,4096]{2,1,0:T(8,128)(2,1)} %local_factor.1, bf16[256,8192]{1,0:T(8,128)(2,1)} %coarse_factor.1), custom_call_target="tpu_custom_call" | custom-call | tf_op jit(solution)/shard_map/pallas_call | solution.py:324
  33.8 0.6 %copy.8 = f32[2,3072]{1,0:T(2,128)} copy(f32[2,3072]{1,0:T(2,128)S(1)} %bitcast.7) | data formatting | bytes 49152

commit v5 on v4

--- a/solution.py
+++ b/solution.py
@@ -35,7 +35,7 @@
     sizes,
     margin, aggregate, residual, local_factor, coarse_factor,
     out,
-    margin_v, agg_v, agg_s, res_v, w_v, v_v, mine, pick_out, pick_in, c_out, c_in, c_full, halo, inner_v,
+    margin_v, agg_v, agg_s, res_v, w_v, v_v, vt_v, mine, pick_out, pick_in, c_out, c_in, c_full, halo, inner_v,
     part_h, recv_h, part_o, recv_o, back, e_part, e_recv, e_full, acc,
     fence, load_sem, pick_send, pick_recv, cs_send, cs_recv, ca_send, ca_recv, halo_send, halo_recv,
     h_send, h_recv, o_send, o_recv, back_send, back_recv, es_send, es_recv, ea_send, ea_recv,
@@ -166,6 +166,20 @@
     for i in range(inner_tiles):
         inner_v[i * deep : (i + 1) * deep, :] = inner[:, i * BLK : (i + 1) * BLK]
 
+    load_v.wait()
+    tile = 2 * BLK
+    panel_tiles = v_v.shape[1] // tile
+
+    def transpose_tiles(begin, end):
+        def one(n, carry):
+            at = pl.ds(pl.multiple_of(n * tile, tile), tile)
+            vt_v[at, :] = v_v[:, at].T
+            return carry
+
+        lax.fori_loop(begin, end, one, 0)
+
+    transpose_tiles(0, panel_tiles // 2)
+
     wait_all(pick_in.at[pl.ds(0, n_sub - 1)], pick_recv)
     pick_in[me] = jnp.zeros((hr, BLK), F32)
     halo[pl.ds(grp * hr, hr)] = jnp.sum(pick_in[...], axis=0)
@@ -183,6 +197,7 @@
             c_full[me * per + i, r : r + 1, :] = coarse[i : i + 1, r * BLK : (r + 1) * BLK]
     mine_c = c_full.at[pl.ds(me * per, per)]
     to_plane(lambda t: mine_c, mine_c, ca_send, ca_recv)
+    transpose_tiles(panel_tiles // 2, panel_tiles)
 
     wait_all(halo.at[pl.ds(0, (n_grp - 1) * hr)], halo_recv)
     halo_rhs = jnp.concatenate(
@@ -228,19 +243,15 @@
     )
 
     wait_all(c_full.at[pl.ds(0, ncb - per)], ca_recv)
-    load_v.wait()
     c_rows = jnp.concatenate([c_full[j] for j in range(ncb)], axis=1).astype(BF16)
-    panel = v_v.shape[0]
+    half = v_v.shape[0] // 2
     inner_c = jnp.concatenate(
         [
-            lax.dot_general(
-                c_rows, v_v[first : first + panel // 2, :], NT, preferred_element_type=F32
-            )
-            for first in (0, panel // 2)
+            jnp.dot(c_rows, vt_v[:, at : at + half], preferred_element_type=F32)
+            for at in (0, half)
         ],
         axis=1,
     ).astype(BF16)
-    fenced()
     e_mine = jnp.dot(inner_c, v_v[...], preferred_element_type=F32)
     for j in range(ncb):
         e_part[j] = e_mine[:, j * BLK : (j + 1) * BLK]
@@ -267,15 +278,6 @@
     wait_all(recv_o.at[pl.ds(0, (n_grp - 1) * orr)], o_recv)
     recv_o[pl.ds(grp * orr, orr)] = part_o[pl.ds(grp * orr, orr)]
     total = jnp.sum(recv_o[...].reshape(n_grp, orr, BLK), axis=0)
-    wait_all(e_full.at[pl.ds(0, ncb - per)], ea_recv)
-    load_ids.wait()
-    for b in range(own):
-        acc[b * rows : (b + 1) * rows, :] = e_full[agg_s[0, b]]
-    for r in range(rows):
-        acc[pl.ds(r, own, stride=rows), :] = (
-            acc[pl.ds(r, own, stride=rows), :] + total[r * own : (r + 1) * own, :]
-        )
-
     wait_all(back.at[pl.ds(0, (n_sub - 1) * hr)], back_recv)
     values = jnp.concatenate(
         [
@@ -293,9 +295,15 @@
     )
     returned = split_dot(owner_hot.astype(BF16), values)
     for r in range(rows):
-        out[pl.ds(r, own, stride=rows), :] = (
-            acc[pl.ds(r, own, stride=rows), :] + returned[:, r * BLK : (r + 1) * BLK]
+        acc[pl.ds(r, own, stride=rows), :] = (
+            total[r * own : (r + 1) * own, :] + returned[:, r * BLK : (r + 1) * BLK]
         )
+    load_ids.wait()
+    wait_all(e_full.at[pl.ds(0, ncb - per)], ea_recv)
+    for b in range(own):
+        j = agg_s[0, b]
+        at = slice(b * rows, (b + 1) * rows)
+        out[at, :] = acc[at, :] + e_full[j]
 
     wait_all(pick_in.at[pl.ds(0, n_sub - 1)], pick_send)
     wait_all(c_in.at[pl.ds(0, n_sub - 1)], cs_send)
@@ -339,6 +347,7 @@
             vm((own * rhs, BLK), F32),
             vm((inner, own_width + margins * BLK), BF16),
             vm(coarse_factor.shape, BF16),
+            vm(coarse_factor.shape[::-1], BF16),
             vm((rows * own, BLK), F32),
             vm((n_sub * rows * margins, BLK), F32),
             vm((n_sub, rows * margins, BLK), F32),

time: 34.5 us -> 33.8 us (0.980)
  Pallas kernels: 33.8 us -> 33.1 us
    pallas_call x1, Pallas kernels: 33.8 us -> 33.1 us  [on_device(): pl.pallas_call(functools.partial(kernel, sizes), out_shape=pltpu.VMEM((ro...]
where the time goes in v5:
time: 33.8 us; the launch traced here: 33.7 us
  Pallas kernels  33.1 us (98%)
  local copies, waits for them, and re-layouts  0.61 us (2%)
    pallas_call x1, Pallas kernels, on_device(): pl.pallas_call(functools.partial(kernel, sizes), out_shape=pltpu.VMEM((ro...  33.1 us

profile of v5, /device:TPU:1, one launch (start us, length us, event | category | flops | bytes accessed | tf_op | source)
XLA Modules:
  0.0 33.7 jit_solution(4034683596727601884)
XLA Ops:
  0.0 33.1 %shard_map.55 = f32[48,128]{1,0:T(8,128)S(1)} custom-call(s32[8,32]{1,0:T(8,128)} %bitcast.8, s32[1,24]{1,0:T(1,128)} %bitcast.9, f32[16,3072]{1,0:T(8,128)} %residual.1, bf16[1,512,4096]{2,1,0:T(8,128)(2,1)} %local_factor.1, bf16[256,8192]{1,0:T(8,128)(2,1)} %coarse_factor.1), custom_call_target="tpu_custom_call" | custom-call | tf_op jit(solution)/shard_map/pallas_call | solution.py:332
  33.1 0.6 %copy.8 = f32[2,3072]{1,0:T(2,128)} copy(f32[2,3072]{1,0:T(2,128)S(1)} %bitcast.7) | data formatting | bytes 49152

commit v6 on v5

--- a/solution.py
+++ b/solution.py
@@ -35,9 +35,9 @@
     sizes,
     margin, aggregate, residual, local_factor, coarse_factor,
     out,
-    margin_v, agg_v, agg_s, res_v, w_v, v_v, vt_v, mine, pick_out, pick_in, c_out, c_in, c_full, halo, inner_v,
+    margin_v, agg_v, agg_s, res_v, w_v, v_v, vt_v, wt_v, mine, pick_out, pick_in, c_out, c_in, c_full, halo, inner_v,
     part_h, recv_h, part_o, recv_o, back, e_part, e_recv, e_full, acc,
-    fence, load_sem, pick_send, pick_recv, cs_send, cs_recv, ca_send, ca_recv, halo_send, halo_recv,
+    load_sem, pick_send, pick_recv, cs_send, cs_recv, ca_send, ca_recv, halo_send, halo_recv,
     h_send, h_recv, o_send, o_recv, back_send, back_recv, es_send, es_recv, ea_send, ea_recv,
 ):
     n_sub, n_grp, own, margins, ncb = sizes
@@ -66,7 +66,10 @@
     column = [
         (lax.rem(grp + d, n_grp), me) for d in sorted(range(1, n_grp), key=lambda d: -far(d, n_grp))
     ]
-    for target in plane + column:
+    far_z = [far(d, n_grp) for d in sorted(range(1, n_grp), key=lambda d: -far(d, n_grp))]
+    far_p = [far(dx, nx) + far(dy, ny) for dx, dy, _ in steps]
+    ranked = sorted(zip(far_z + far_p, range(len(far_z + far_p))), key=lambda t: -t[0])
+    for target in [(column + plane)[i] for _, i in ranked]:
         pl.semaphore_signal(barrier, inc=1, device_id=target, device_id_type=MESH)
 
     load_margin = pltpu.make_async_copy(margin, margin_v, load_sem.at[3])
@@ -99,10 +102,6 @@
                 src_ref=src(target[0]), dst_ref=dst, send_sem=send, recv_sem=recv,
                 device_id=target, device_id_type=MESH,
             ).start()
-
-    def fenced():
-        pl.semaphore_signal(fence, 1)
-        pl.semaphore_wait(fence, 1)
 
     slots = n_sub * margins
     each = BLK // n_sub
@@ -166,6 +165,10 @@
     for i in range(inner_tiles):
         inner_v[i * deep : (i + 1) * deep, :] = inner[:, i * BLK : (i + 1) * BLK]
 
+    for k in range(0, margins, 2):
+        at = k * BLK
+        wt_v[at : at + 2 * BLK, :] = w_v[:, width + at : width + at + 2 * BLK].T
+
     load_v.wait()
     tile = 2 * BLK
     panel_tiles = v_v.shape[1] // tile
@@ -226,9 +229,8 @@
         ],
         axis=0,
     )
-    inner = inner + lax.dot_general(halo_rhs, w_v[:, width:], NT, preferred_element_type=F32)
+    inner = inner + jnp.dot(halo_rhs, wt_v[...], preferred_element_type=F32)
     inner = inner.astype(BF16)
-    fenced()
 
     def scatter_rows(sol, dst, blocks_each):
         for r in range(rows):
@@ -348,6 +350,7 @@
             vm((inner, own_width + margins * BLK), BF16),
             vm(coarse_factor.shape, BF16),
             vm(coarse_factor.shape[::-1], BF16),
+            vm((margins * BLK, inner), BF16),
             vm((rows * own, BLK), F32),
             vm((n_sub * rows * margins, BLK), F32),
             vm((n_sub, rows * margins, BLK), F32),
@@ -365,7 +368,6 @@
             vm((n_sub, per, rows, BLK), F32),
             vm((ncb, rows, BLK), F32),
             vm((rows * own, BLK), F32),
-            pltpu.SemaphoreType.REGULAR,
             sem((6,)),
         ] + [sem] * 18,
         compiler_params=pltpu.CompilerParams(collective_id=0, has_side_effects=True),

time: 33.8 us -> 33.4 us (0.988)
  Pallas kernels: 33.1 us -> 32.7 us
    pallas_call x1, Pallas kernels: 33.1 us -> 32.7 us  [on_device(): pl.pallas_call(functools.partial(kernel, sizes), out_shape=pltpu.VMEM((ro...]
where the time goes in v6:
time: 33.4 us; the launch traced here: 33.3 us
  Pallas kernels  32.7 us (98%)
  local copies, waits for them, and re-layouts  0.61 us (2%)
    pallas_call x1, Pallas kernels, on_device(): pl.pallas_call(functools.partial(kernel, sizes), out_shape=pltpu.VMEM((ro...  32.7 us

profile of v6, /device:TPU:1, one launch (start us, length us, event | category | flops | bytes accessed | tf_op | source)
XLA Modules:
  0.0 33.3 jit_solution(10342593555188346475)
XLA Ops:
  0.0 32.7 %shard_map.55 = f32[48,128]{1,0:T(8,128)S(1)} custom-call(s32[8,32]{1,0:T(8,128)} %bitcast.8, s32[1,24]{1,0:T(1,128)} %bitcast.9, f32[16,3072]{1,0:T(8,128)} %residual.1, bf16[1,512,4096]{2,1,0:T(8,128)(2,1)} %local_factor.1, bf16[256,8192]{1,0:T(8,128)(2,1)} %coarse_factor.1), custom_call_target="tpu_custom_call" | custom-call | tf_op jit(solution)/shard_map/pallas_call | solution.py:334
  32.7 0.6 %copy.8 = f32[2,3072]{1,0:T(2,128)} copy(f32[2,3072]{1,0:T(2,128)S(1)} %bitcast.7) | data formatting | bytes 49152

commit v7 on v6

--- a/solution.py
+++ b/solution.py
@@ -181,7 +181,7 @@
 
         lax.fori_loop(begin, end, one, 0)
 
-    transpose_tiles(0, panel_tiles // 2)
+    transpose_tiles(0, panel_tiles * 3 // 4)
 
     wait_all(pick_in.at[pl.ds(0, n_sub - 1)], pick_recv)
     pick_in[me] = jnp.zeros((hr, BLK), F32)
@@ -200,7 +200,7 @@
             c_full[me * per + i, r : r + 1, :] = coarse[i : i + 1, r * BLK : (r + 1) * BLK]
     mine_c = c_full.at[pl.ds(me * per, per)]
     to_plane(lambda t: mine_c, mine_c, ca_send, ca_recv)
-    transpose_tiles(panel_tiles // 2, panel_tiles)
+    transpose_tiles(panel_tiles * 3 // 4, panel_tiles)
 
     wait_all(halo.at[pl.ds(0, (n_grp - 1) * hr)], halo_recv)
     halo_rhs = jnp.concatenate(

time: 33.4 us -> 33.4 us (level)
  no operation moved by 1% of the time
where the time goes in v7:
time: 33.4 us; the launch traced here: 33.3 us
  Pallas kernels  32.7 us (98%)
  local copies, waits for them, and re-layouts  0.61 us (2%)
    pallas_call x1, Pallas kernels, on_device(): pl.pallas_call(functools.partial(kernel, sizes), out_shape=pltpu.VMEM((ro...  32.7 us

profile of v7, /device:TPU:1, one launch (start us, length us, event | category | flops | bytes accessed | tf_op | source)
XLA Modules:
  0.0 33.3 jit_solution(5319079646726401764)
XLA Ops:
  0.0 32.7 %shard_map.55 = f32[48,128]{1,0:T(8,128)S(1)} custom-call(s32[8,32]{1,0:T(8,128)} %bitcast.8, s32[1,24]{1,0:T(1,128)} %bitcast.9, f32[16,3072]{1,0:T(8,128)} %residual.1, bf16[1,512,4096]{2,1,0:T(8,128)(2,1)} %local_factor.1, bf16[256,8192]{1,0:T(8,128)(2,1)} %coarse_factor.1), custom_call_target="tpu_custom_call" | custom-call | tf_op jit(solution)/shard_map/pallas_call | solution.py:334
  32.7 0.6 %copy.8 = f32[2,3072]{1,0:T(2,128)} copy(f32[2,3072]{1,0:T(2,128)S(1)} %bitcast.7) | data formatting | bytes 49152

commit v8 on v6

--- a/solution.py
+++ b/solution.py
@@ -259,17 +259,17 @@
         e_part[j] = e_mine[:, j * BLK : (j + 1) * BLK]
     to_plane(lambda t: e_part.at[pl.ds(t * per, per)], e_recv.at[me], es_send, es_recv)
 
-    scatter_rows(jnp.dot(inner, w_v[:, :width], preferred_element_type=F32), part_o, own)
-    orr = rows * own
-    to_column(
-        lambda t: part_o.at[pl.ds(t * orr, orr)], recv_o.at[pl.ds(grp * orr, orr)], o_send, o_recv
-    )
-
     wait_all(recv_h.at[pl.ds(0, (n_grp - 1) * hr)], h_recv)
     recv_h[pl.ds(grp * hr, hr)] = part_h[pl.ds(grp * hr, hr)]
     mine_back = back.at[pl.ds(me * hr, hr)]
     back[pl.ds(me * hr, hr)] = jnp.sum(recv_h[...].reshape(n_grp, hr, BLK), axis=0)
     to_plane(lambda t: mine_back, mine_back, back_send, back_recv)
+
+    scatter_rows(jnp.dot(inner, w_v[:, :width], preferred_element_type=F32), part_o, own)
+    orr = rows * own
+    to_column(
+        lambda t: part_o.at[pl.ds(t * orr, orr)], recv_o.at[pl.ds(grp * orr, orr)], o_send, o_recv
+    )
 
     wait_all(e_recv.at[pl.ds(0, n_sub - 1)], es_recv)
     e_recv[me] = e_part[pl.ds(me * per, per)]

time: 33.4 us -> 33.4 us (level)
  no operation moved by 1% of the time
where the time goes in v8:
time: 33.4 us; the launch traced here: 33.3 us
  Pallas kernels  32.7 us (98%)
  local copies, waits for them, and re-layouts  0.61 us (2%)
    pallas_call x1, Pallas kernels, on_device(): pl.pallas_call(functools.partial(kernel, sizes), out_shape=pltpu.VMEM((ro...  32.7 us

profile of v8, /device:TPU:1, one launch (start us, length us, event | category | flops | bytes accessed | tf_op | source)
XLA Modules:
  0.0 33.3 jit_solution(15361492374022006620)
XLA Ops:
  0.0 32.7 %shard_map.55 = f32[48,128]{1,0:T(8,128)S(1)} custom-call(s32[8,32]{1,0:T(8,128)} %bitcast.8, s32[1,24]{1,0:T(1,128)} %bitcast.9, f32[16,3072]{1,0:T(8,128)} %residual.1, bf16[1,512,4096]{2,1,0:T(8,128)(2,1)} %local_factor.1, bf16[256,8192]{1,0:T(8,128)(2,1)} %coarse_factor.1), custom_call_target="tpu_custom_call" | custom-call | tf_op jit(solution)/shard_map/pallas_call | solution.py:334
  32.7 0.6 %copy.8 = f32[2,3072]{1,0:T(2,128)} copy(f32[2,3072]{1,0:T(2,128)S(1)} %bitcast.7) | data formatting | bytes 49152
